TPU v7x, 32 devices: a whole 2x2x4 slice. The times are simulated.
32 devices in a mesh: group: 2 (over y), blk: 4 (over z), gz: 2 (over x), view: 2 (over core).
Axes of the slice: x: 2, y: 2, z: 4, core: 2. Of those that a mesh axis runs over, the one named last changes fastest.
Arguments:
- estimate: float32 [32, 128, 128], P(('group', 'gz'), 'blk'), parts along dimension 0, may hold values from 0.5 to 2
- view_tiles: bfloat16 [192, 14, 14, 128], P(('group', 'blk', 'gz', 'view')), parts along dimension 0, may hold values from 0.25 to 4
- tile_pairs: int32 [192, 2], P('group'), parts along dimension 0, may hold values from 0 to 31, as said below
- kernel_table: bfloat16 [6, 16, 7, 7, 7], P('view', ('group', 'blk', 'gz')), parts along dimension 1, may hold values from 0.0014953613 to 0.0059814453
- kernel_ids: int32 [64, 6], P('group'), parts along dimension 0, may hold values from 0 to 7
Outputs:
- estimate_out: float32 [32, 128, 128], P(('group', 'gz'), 'blk'), parts along dimension 0
There are 2 independent parts, one for each index of `group`. A program takes and returns all parts, laid end to end along the dimension named above; each array names one. Nothing has to cross between parts.
Inputs may be any that keep to these rules, and one draw needn't show every extreme that they name: Tile t is stored on the device at position t // 6 in the order blk, gz, view. Its block b = tile_pairs[t, 0] lies in that device's sub-slab (b // 16 is its gz index) and its view tile_pairs[t, 1] in that device's half (view // 3 is its view index). No block has two tiles of one view; every block has at least one tile of each half of the views. The tiles of one device go to at most 3 tiles' worth of blocks with the same (b % 16) // 4, and some device reaches 3; the blocks of one sub-slab with the same (b % 16) // 4 have at most 12 tiles of one half of the views, and some reach it.
All inputs are finite; a program needn't handle non-finite values.
Results may differ from a plain program's by a relative error of at most 0.0003.
Values may be sent and summed in bfloat16 or wider, within the bound.
No kernel may reach another device: no remote copies, remote signals or barrier semaphores. Data moves between devices by JAX's collectives and lax.ppermute only.
A program may use at most 64 MiB of HBM per device.

v0:
```python
import jax
import jax.numpy as jnp
from jax import lax
from jax.sharding import PartitionSpec as P

ITERS = 2


def extended_2(array, sides, width):
    for axis, dim in sides:
        peers, length = (lax.axis_size(axis), array.shape[dim])
        up = [(i, (i + 1) % peers) for i in range(peers - 1)]
        down = [(j, i) for i, j in up]
        last = lax.slice_in_dim(array, length - width, length, axis=dim)
        leading = lax.slice_in_dim(array, 0, width, axis=dim)
        before = lax.ppermute(last, axis, up)
        after = lax.ppermute(leading, axis, down)
        array = jnp.concatenate([before, array, after], axis=dim)
    return array


def toeplitz_pair(kernel, cells_x):
    kernel_size = kernel.shape[0]
    kernel_reach = (kernel_size - 1) // 2
    row_index = jnp.arange(cells_x, dtype=jnp.int32)[:, None]
    column_index = jnp.arange(cells_x, dtype=jnp.int32)[None, :]
    tap_index = jnp.arange(kernel_size, dtype=jnp.int32)[:, None, None]
    forward_mask = ((row_index - column_index + kernel_reach)[None] == tap_index).astype(
        jnp.bfloat16
    )
    backward_mask = ((column_index - row_index + kernel_reach)[None] == tap_index).astype(
        jnp.bfloat16
    )
    forward = jnp.einsum(
        "abc,cji->abji", kernel, forward_mask, preferred_element_type=jnp.float32
    ).astype(jnp.bfloat16)
    backward = jnp.einsum(
        "abc,cji->abji", kernel, backward_mask, preferred_element_type=jnp.float32
    ).astype(jnp.bfloat16)
    return (
        forward.reshape(kernel_size, kernel_size * cells_x, cells_x),
        backward.reshape(kernel_size, kernel_size * cells_x, cells_x),
    )


def blurring(extended, forward, extent_z, extent_y):
    kernel_size = forward.shape[0]
    cells_x = extended.shape[2]
    shifted = jnp.stack(
        [extended[:, shift_y : shift_y + extent_y, :] for shift_y in range(kernel_size)], axis=2
    )
    shifted = shifted.reshape(extended.shape[0], extent_y, kernel_size * cells_x)
    accumulated = jnp.zeros((extent_z * extent_y, cells_x), jnp.float32)
    for plane_z in range(kernel_size):
        matrix_rows = shifted[plane_z : plane_z + extent_z].reshape(
            extent_z * extent_y, kernel_size * cells_x
        )
        accumulated = accumulated + jnp.dot(
            matrix_rows, forward[plane_z], preferred_element_type=jnp.float32
        )
    return accumulated.reshape(extent_z, extent_y, cells_x)


def spread(ratio, backward, extent_z, extent_y):
    kernel_size = backward.shape[0]
    kernel_reach = (kernel_size - 1) // 2
    cells_x = ratio.shape[2]
    shifted = jnp.stack(
        [
            ratio[:, 2 * kernel_reach - shift_y : 2 * kernel_reach - shift_y + extent_y, :]
            for shift_y in range(kernel_size)
        ],
        axis=2,
    )
    shifted = shifted.reshape(ratio.shape[0], extent_y, kernel_size * cells_x)
    accumulated = jnp.zeros((extent_z * extent_y, cells_x), jnp.float32)
    for plane_z in range(kernel_size):
        begin_z = 2 * kernel_reach - plane_z
        matrix_rows = shifted[begin_z : begin_z + extent_z].reshape(
            extent_z * extent_y, kernel_size * cells_x
        )
        accumulated = accumulated + jnp.dot(
            matrix_rows, backward[plane_z], preferred_element_type=jnp.float32
        )
    return accumulated.reshape(extent_z, extent_y, cells_x)


def tile_correction(one_tile, extended, kernel, first_z, first_y, volume_z, volume_y):
    extent_z, extent_y, cells_x = one_tile.shape
    kernel_reach = (kernel.shape[0] - 1) // 2
    forward, backward = toeplitz_pair(kernel, cells_x)
    blurred = blurring(extended, forward, extent_z, extent_y)
    cell_z = first_z + jnp.arange(extent_z, dtype=jnp.int32) - kernel_reach
    cell_y = first_y + jnp.arange(extent_y, dtype=jnp.int32) - kernel_reach
    inside = ((cell_z >= 0) & (cell_z < volume_z))[:, None, None] & (
        (cell_y >= 0) & (cell_y < volume_y)
    )[None, :, None]
    ratio = jnp.where(inside, one_tile.astype(jnp.float32) / blurred, 0.0).astype(jnp.bfloat16)
    return spread(ratio, backward, extent_z - 2 * kernel_reach, extent_y - 2 * kernel_reach)


def on_device(estimate, view_tiles, tile_pairs, kernel_table, kernel_ids):
    cells_z, local_y, cells_x = estimate.shape
    tile_count = view_tiles.shape[0]
    extent_y = view_tiles.shape[2]
    views_here = kernel_table.shape[0]
    kernel_reach = (kernel_table.shape[2] - 1) // 2
    block_cells = extent_y - 2 * kernel_reach
    blocks_here = local_y // block_cells
    block_devices = lax.axis_size("blk")
    slab_devices = lax.axis_size("gz")
    core_devices = lax.axis_size("view")
    block_rank = lax.axis_index("blk")
    slab_rank = lax.axis_index("gz")
    core_rank = lax.axis_index("view")
    volume_z = cells_z * slab_devices
    volume_y = local_y * block_devices
    blocks_row = blocks_here * block_devices
    slot_count = (views_here * blocks_here + block_devices - 1) // block_devices
    home_most = views_here * blocks_here
    device_total = block_devices * slab_devices * core_devices
    tile_total = tile_pairs.shape[0]
    kernels = lax.all_gather(kernel_table, ("blk", "gz"), axis=1, tiled=True)
    tile_block = tile_pairs[:, 0]
    tile_view = tile_pairs[:, 1]
    tile_ids = jnp.arange(tile_total, dtype=jnp.int32)
    block_row = tile_block % blocks_row
    home_group = block_row // blocks_here
    home_slab = tile_block // blocks_row
    in_block = block_row % blocks_here
    stored_group = tile_ids // tile_count // (slab_devices * core_devices)
    grouped = home_group.reshape(device_total, tile_count)
    earlier = jnp.arange(tile_count)[:, None] > jnp.arange(tile_count)[None, :]
    slot_rank = jnp.sum(
        ((grouped[:, :, None] == grouped[:, None, :]) & earlier[None]).astype(jnp.int32), axis=2
    ).reshape(-1)
    is_mine = (
        (home_slab == slab_rank)
        & (home_group == block_rank)
        & (tile_view // views_here == core_rank)
    )
    listed = jnp.argsort(jnp.where(is_mine, tile_ids, tile_ids + tile_total))[:home_most]
    live_count = jnp.sum(is_mine.astype(jnp.int32))
    list_source = stored_group[listed]
    list_rank = slot_rank[listed]
    list_block = tile_block[listed]
    list_view = tile_view[listed]
    list_local = in_block[listed]
    first_block = slab_rank * blocks_row + block_rank * blocks_here
    coverage = jnp.sum(
        (tile_block[None, :] == first_block + jnp.arange(blocks_here)[:, None]).astype(jnp.float32),
        axis=1,
    )
    count_field = jnp.repeat(coverage, block_cells)[None, :, None]
    own_ids = (
        block_rank * slab_devices * core_devices + slab_rank * core_devices + core_rank
    ) * tile_count + jnp.arange(tile_count, dtype=jnp.int32)

    def correction_for(one_tile, extended, block_id, view_id):
        kernel = kernels[view_id - core_rank * views_here, kernel_ids[block_id, view_id]]
        first_z = block_id // blocks_row * cells_z
        first_y = block_id % blocks_row * block_cells
        return tile_correction(one_tile, extended, kernel, first_z, first_y, volume_z, volume_y)

    outgoing = jnp.zeros((block_devices, slot_count) + view_tiles.shape[1:], view_tiles.dtype)
    outgoing = outgoing.at[home_group[own_ids], slot_rank[own_ids]].set(view_tiles)
    arrived = lax.all_to_all(outgoing, "blk", split_axis=0, concat_axis=0, tiled=True)
    arrived = arrived.reshape((block_devices * slot_count,) + view_tiles.shape[1:])
    current = estimate
    for iteration in range(ITERS):
        padded = extended_2(current.astype(jnp.bfloat16), (("blk", 1), ("gz", 0)), 2 * kernel_reach)

        def visit_tile(position, summed):
            block_local = list_local[position]
            one_tile = lax.dynamic_index_in_dim(
                arrived, list_source[position] * slot_count + list_rank[position], 0, keepdims=False
            )
            extended = lax.dynamic_slice_in_dim(
                padded, block_local * block_cells, block_cells + 4 * kernel_reach, 1
            )
            correction = correction_for(
                one_tile, extended, list_block[position], list_view[position]
            )
            offset = block_local * block_cells
            window = lax.dynamic_slice_in_dim(summed, offset, block_cells, 1)
            return lax.dynamic_update_slice_in_dim(summed, window + correction, offset, 1)

        summed = lax.fori_loop(0, live_count, visit_tile, jnp.zeros(estimate.shape, jnp.float32))
        combined = lax.psum(summed, "view")
        current = current * combined / count_field
    return current


def solution(mesh):
    in_specs = (
        P(("group", "gz"), "blk", None),
        P(("group", "blk", "gz", "view"), None, None, None),
        P("group", None),
        P("view", ("group", "blk", "gz"), None, None, None),
        P("group", None),
    )
    out_specs = P(("group", "gz"), "blk", None)
    return jax.shard_map(
        on_device, mesh=mesh, in_specs=in_specs, out_specs=out_specs, check_vma=False
    )
```

profile of v0, /device:TPU:0, one launch (start us, length us, event | category | flops | bytes accessed | tf_op | source)
XLA Modules:
  0.0 753.4 jit_solution(275208694247272833)
XLA Ops:
  10.9 2.4 scatter_fusion
  13.2 6.3 all-to-all-start
  19.6 3.9 collective-permute-start
  25.6 2.5 sort.17
  31.3 3.4 collective-permute-start.2
  36.7 36.9 %all_gather.3 = bf16[3,8,7,7,7]{4,3,2,1,0:T(8,128)(2,1)} all-gather(bf16[3,1,7,7,7]{4,3,2,1,0:T(8,128)(2,1)S(1)} %copy-done.4), channel_id=1, replica_groups=mesh['group'=2,'blk'=4,'gz'=2,'view'=2] {'blk','gz'}, dimensions={1}, use_global_device_ids=true | all-gather | bytes 18522 | tf_op jit(solution)/shard_map/all_gather | solution.py:123
  73.7 310.3 %while.26 = (s32[]{:T(128)}, f32[8,32,128]{2,1,0:T(8,128)S(1)}, s32[]{:T(128)}, s32[12]{0:T(128)S(1)}, s32[12]{0:T(128)S(1)}, /*index=5*/s32[12]{0:T(128)S(1)}, ...) while((s32[]{:T(128)}, f32[8,32,128]{2,1,0:T(8,128)S(1)}, ...), condition=%wide.region_5.6_spmd, body=%wide.region_4.5_spmd.sunk | while | flops 442152288 | bytes 46343604 | solution.py:188
  136.8 1.3 convolution_convert_fusion.9
  162.7 1.3 convolution_convert_fusion.9
  188.5 1.3 convolution_convert_fusion.9
  240.1 1.3 convolution_convert_fusion.9
  265.9 1.3 convolution_convert_fusion.9
  385.1 17.2 %all-reduce.3.cloned.1.call-done = f32[8,32,128]{2,1,0:T(8,128)} async-done(((f32[8,32,128]{2,1,0:T(8,128)}), f32[8,32,128]{2,1,0:T(8,128)}) %all-reduce.3.cloned.1.call-update) | async-done | bytes 131088 | tf_op jit(solution)/shard_map/psum | solution.py:189
  403.4 3.7 collective-permute-start.4
  408.5 4.2 collective-permute-done.5
  412.8 3.4 collective-permute-start.6
  418.1 4.3 collective-permute-done.7
  422.4 305.3 %while.27 = (s32[]{:T(128)}, f32[8,32,128]{2,1,0:T(8,128)S(1)}, s32[]{:T(128)}, s32[12]{0:T(128)S(1)}, s32[12]{0:T(128)S(1)}, /*index=5*/s32[12]{0:T(128)S(1)}, ...) while((s32[]{:T(128)}, f32[8,32,128]{2,1,0:T(8,128)S(1)}, ...), condition=%wide.region_9.10_spmd, body=%wide.region_8.9_spmd.sunk | while | flops 442152288 | bytes 46343604 | solution.py:188
  430.2 1.4 dynamic_slice.198
  455.6 1.4 dynamic_slice.198
  481.0 1.4 dynamic_slice.198
  506.3 1.4 dynamic_slice.198
  531.7 1.4 dynamic_slice.198
  557.1 1.4 dynamic_slice.198
  582.4 1.4 dynamic_slice.198
  607.8 1.4 dynamic_slice.198
  633.2 1.4 dynamic_slice.198
  658.6 1.4 dynamic_slice.198
  683.9 1.4 dynamic_slice.198
  709.3 1.4 dynamic_slice.198
  728.5 16.3 %all-reduce.5.cloned.1.call-done = f32[8,32,128]{2,1,0:T(8,128)} async-done(((f32[8,32,128]{2,1,0:T(8,128)}), f32[8,32,128]{2,1,0:T(8,128)}) %all-reduce.5.cloned.1.call-update) | async-done | bytes 131088 | tf_op jit(solution)/shard_map/psum | solution.py:189
  744.8 1.7 multiply_divide_fusion
  (1969 shorter events, 349.1 us)
Async XLA Ops:
  6.5 4.3 copy-start.3
  9.2 10.3 %copy-start.2 = (f32[8,32,128]{2,1,0:T(8,128)S(1)}, f32[8,32,128]{2,1,0:T(8,128)}, u32[]{:S(2)}) copy-start(f32[8,32,128]{2,1,0:T(8,128)} %param.9) | copy-start | bytes 393220
  13.2 60.5 %all-to-all-start = ((bf16[4,3,14,14,128]{4,3,2,1,0:T(8,128)(2,1)}), bf16[4,3,14,14,128]{4,3,2,1,0:T(8,128)(2,1)}, u32[]{:S(2)}, u32[]{:S(2)}) async-start(bf16[4,3,14,14,128]{4,3,2,1,0:T(8,128)(2,1)} %scatter_fusion), calls=%async_computation | async-start | bytes 1376256 | tf_op jit(solution)/shard_map/all_to_all | solution.py:167
  19.6 17.1 %copy-start.4 = (bf16[3,1,7,7,7]{4,3,2,1,0:T(8,128)(2,1)S(1)}, bf16[3,1,7,7,7]{4,3,2,1,0:T(8,128)(2,1)}, u32[]{:S(2)}) copy-start(bf16[3,1,7,7,7]{4,3,2,1,0:T(8,128)(2,1)} %param.12) | copy-start | bytes 6178
  19.6 382.8 %all-reduce.3.cloned.1.call-start = ((), (), s32[]{:S(2)}) async-start(), calls=%async_computation.1 | async-start | bytes 262144 | tf_op jit(solution)/shard_map/psum | solution.py:189
  19.6 11.6 %collective-permute-start = (bf16[8,6,128]{2,1,0:T(8,128)(2,1)S(1)}, bf16[8,6,128]{2,1,0:T(8,128)(2,1)S(1)}, u32[]{:S(2)}, u32[]{:S(2)}) collective-permute-start(bf16[8,6,128]{2,1,0:T(8,128)(2,1)S(1)} %get-tuple-element.543), channel_id=1, source_target_pairs={{0,4},{4,8},{8,12},{1,5},{5,9},{9,13},{2,6},{6,10},{10,14},{3,7},{... | collective-permute-start | bytes 36872 | tf_op jit(solution)/shard_map/ppermute | solution.py:16
  23.6 7.6 %collective-permute-start.1 = (bf16[8,6,128]{2,1,0:T(8,128)(2,1)S(1)}, bf16[8,6,128]{2,1,0:T(8,128)(2,1)S(1)}, u32[]{:S(2)}, u32[]{:S(2)}) collective-permute-start(bf16[8,6,128]{2,1,0:T(8,128)(2,1)S(1)} %get-tuple-element.544), channel_id=1, source_target_pairs={{4,0},{8,4},{12,8},{5,1},{9,5},{13,9},{6,2},{10,6},{14,10},{7,3},{... | collective-permute-start | bytes 36872 | tf_op jit(solution)/shard_map/ppermute | solution.py:17
  31.3 42.4 %collective-permute-start.2 = (bf16[6,44,128]{2,1,0:T(8,128)(2,1)S(1)}, bf16[6,44,128]{2,1,0:T(8,128)(2,1)S(1)}, u32[]{:S(2)}, u32[]{:S(2)}) collective-permute-start(bf16[6,44,128]{2,1,0:T(8,128)(2,1)S(1)} %get-tuple-element.539), channel_id=1, source_target_pairs={{0,2},{1,3},{4,6},{5,7},{8,10},{9,11},{12,14},{13,15},{16,18},{17,... | collective-permute-start | bytes 202760 | tf_op jit(solution)/shard_map/ppermute | solution.py:16
  34.7 38.9 %collective-permute-start.3 = (bf16[6,44,128]{2,1,0:T(8,128)(2,1)S(1)}, bf16[6,44,128]{2,1,0:T(8,128)(2,1)S(1)}, u32[]{:S(2)}, u32[]{:S(2)}) collective-permute-start(bf16[6,44,128]{2,1,0:T(8,128)(2,1)S(1)} %get-tuple-element.540), channel_id=1, source_target_pairs={{2,0},{3,1},{6,4},{7,5},{10,8},{11,9},{14,12},{15,13},{18,16},{19,... | collective-permute-start | bytes 202760 | tf_op jit(solution)/shard_map/ppermute | solution.py:17
  384.0 0.7 copy-start.1
  384.7 360.1 %all-reduce.5.cloned.1.call-start = ((), (), s32[]{:S(2)}) async-start(), calls=%async_computation.2 | async-start | bytes 262144 | tf_op jit(solution)/shard_map/psum | solution.py:189
  403.4 5.1 collective-permute-start.4
  407.1 5.6 collective-permute-start.5
  412.8 5.3 collective-permute-start.6
  416.1 6.2 collective-permute-start.7
  727.8 0.7 copy-start
Sparse Core Ops, SparseCore 0:
  384.8 17.4 all-reduce.2
  728.6 16.1 all-reduce.4
where the time goes:
time: 762 us; the launch traced here: 753 us
  loops' own time  261 us (34%)
  local copies, waits for them, and re-layouts  202 us (27%)
  matrix products  138 us (18%)
  waiting for transfers between devices  43.3 us (6%)
  blocking collectives  36.9 us (5%)
  other arithmetic  31.9 us (4%)
  starting transfers between devices  26 us (3%)
  between operations  13.7 us (2%)
    another operation x2, loops' own time, on_device(): lax.fori_loop(0, live_count, visit_tile, jnp.zeros(estimate.shape, jnp.fl...  261 us
    dot_general x168, matrix products, blurring(): jnp.dot(matrix_rows, forward[plane_z], preferred_element_type=jnp.float32)  44.2 us
    all_gather x1, blocking collectives, on_device(): kernels = lax.all_gather(kernel_table, ('blk', 'gz'), axis=1, tiled=True)  36.9 us
    slice x192, local copies, waits for them, and re-layouts, blurring(): shifted[plane_z:plane_z + extent_z]  35.4 us
    psum x2, waiting for transfers between devices, on_device(): combined = lax.psum(summed, 'view')  33.6 us
    dot_general x24, matrix products, toeplitz_pair(): jnp.einsum('abc,cji->abji', kernel, forward_mask, preferred_element_type=...  32.2 us
    dot_general x24, matrix products, toeplitz_pair(): jnp.einsum('abc,cji->abji', kernel, backward_mask, preferred_element_type...  32.2 us
    while x624, local copies, waits for them, and re-layouts  32.1 us
  transfers between devices with their start and end apart: 11, of which 7 were waited for; matrix products, arithmetic and copies ran while one was open for 1% of the time, Pallas kernels for 0%

commit v1 on v0

--- a/solution.py
+++ b/solution.py
@@ -1,9 +1,18 @@
+import functools
 import jax
 import jax.numpy as jnp
 from jax import lax
 from jax.sharding import PartitionSpec as P
+from jax.lax import all_gather
 
 ITERS = 2
+
+
+def wait_face(x_local, device_axis):
+    return jnp.sum(all_gather(x_local, device_axis), axis=0)
+
+
+attach_copies = functools.partial(wait_face, device_axis="view")
 
 
 def extended_2(array, sides, width):
@@ -186,7 +195,7 @@
             return lax.dynamic_update_slice_in_dim(summed, window + correction, offset, 1)
 
         summed = lax.fori_loop(0, live_count, visit_tile, jnp.zeros(estimate.shape, jnp.float32))
-        combined = lax.psum(summed, "view")
+        combined = attach_copies(summed)
         current = current * combined / count_field
     return current
 

time: 762 us -> 721 us (0.946)
  waiting for transfers between devices: 43.3 us -> 9.29 us
  between operations: 13.7 us -> 0.28 us
  loops' own time: 261 us -> 269 us
    psum x2 -> x0, waiting for transfers between devices: 33.6 us -> none  [on_device(): combined = lax.psum(summed, 'view')]
    another operation x2, loops' own time: 261 us -> 269 us  [on_device(): lax.fori_loop(0, live_count, visit_tile, jnp.zeros(estimate.shape, jnp.fl...]
  transfers between devices with their start and end apart: 11 -> 9, of which waited for: 7 -> 4; matrix products, arithmetic and copies ran while one was open for 1% -> 1% of each run, Pallas kernels for 0% -> 0%
where the time goes in v1:
time: 721 us; the launch traced here: 712 us
  loops' own time  269 us (37%)
  local copies, waits for them, and re-layouts  201 us (28%)
  matrix products  139 us (19%)
  blocking collectives  40.7 us (6%)
  other arithmetic  30.9 us (4%)
  starting transfers between devices  21.4 us (3%)
  waiting for transfers between devices  9.29 us (1%)
    another operation x2, loops' own time, on_device(): lax.fori_loop(0, live_count, visit_tile, jnp.zeros(estimate.shape, jnp.fl...  269 us
    dot_general x168, matrix products, blurring(): jnp.dot(matrix_rows, forward[plane_z], preferred_element_type=jnp.float32)  44.3 us
    all_gather x1, blocking collectives, on_device(): kernels = lax.all_gather(kernel_table, ('blk', 'gz'), axis=1, tiled=True)  36.7 us
    slice x192, local copies, waits for them, and re-layouts, blurring(): shifted[plane_z:plane_z + extent_z]  35.4 us
    dot_general x24, matrix products, toeplitz_pair(): jnp.einsum('abc,cji->abji', kernel, backward_mask, preferred_element_type...  32.2 us
    dot_general x24, matrix products, toeplitz_pair(): jnp.einsum('abc,cji->abji', kernel, forward_mask, preferred_element_type=...  32.2 us
    while x624, local copies, waits for them, and re-layouts  32.1 us
    dynamic_slice x24, local copies, waits for them, and re-layouts, correction_for(): kernel_ids[block_id, view_id]  30.6 us
  transfers between devices with their start and end apart: 9, of which 4 were waited for; matrix products, arithmetic and copies ran while one was open for 1% of the time, Pallas kernels for 0%

profile of v1, /device:TPU:0, one launch (start us, length us, event | category | flops | bytes accessed | tf_op | source)
XLA Modules:
  0.0 711.5 jit_solution(10762943060918239111)
XLA Ops:
  4.3 2.4 scatter_fusion
  6.7 6.4 all-to-all-start
  13.1 3.9 collective-permute-start
  18.3 2.5 sort.17
  25.0 3.4 collective-permute-start.2
  30.0 36.7 %all_gather.15 = bf16[3,8,7,7,7]{4,3,2,1,0:T(8,128)(2,1)} all-gather(bf16[3,1,7,7,7]{4,3,2,1,0:T(8,128)(2,1)S(1)} %copy-done.3), channel_id=1, replica_groups=mesh['group'=2,'blk'=4,'gz'=2,'view'=2] {'blk','gz'}, dimensions={1}, use_global_device_ids=true | all-gather | bytes 18522 | tf_op jit(solution)/shard_map/all_gather | solution.py:132
  66.8 311.2 %while.26 = (s32[]{:T(128)}, f32[8,32,128]{2,1,0:T(8,128)S(1)}, s32[]{:T(128)}, s32[12]{0:T(128)S(1)}, s32[12]{0:T(128)S(1)}, /*index=5*/s32[12]{0:T(128)S(1)}, ...) while((s32[]{:T(128)}, f32[8,32,128]{2,1,0:T(8,128)S(1)}, ...), condition=%wide.region_5.6_spmd, body=%wide.region_4.5_spmd.sunk | while | flops 442152288 | bytes 46343604 | solution.py:197
  89.6 1.3 convolution_convert_fusion.8
  104.0 1.3 convolution_convert_fusion.9
  115.5 1.3 convolution_convert_fusion.8
  155.8 1.3 convolution_convert_fusion.9
  167.3 1.3 convolution_convert_fusion.8
  193.1 1.3 convolution_convert_fusion.8
  207.5 1.3 convolution_convert_fusion.9
  219.0 1.3 convolution_convert_fusion.8
  259.3 1.3 convolution_convert_fusion.9
  270.8 1.3 convolution_convert_fusion.8
  296.7 1.3 convolution_convert_fusion.8
  311.1 1.3 convolution_convert_fusion.9
  322.6 1.3 convolution_convert_fusion.8
  362.8 1.3 convolution_convert_fusion.9
  374.3 1.3 convolution_convert_fusion.8
  378.0 2.0 all-gather
  382.9 4.2 collective-permute-done.5
  390.4 4.3 collective-permute-done.7
  394.8 313.1 %while.27 = (s32[]{:T(128)}, f32[8,32,128]{2,1,0:T(8,128)S(1)}, s32[]{:T(128)}, s32[12]{0:T(128)S(1)}, s32[12]{0:T(128)S(1)}, /*index=5*/s32[12]{0:T(128)S(1)}, ...) while((s32[]{:T(128)}, f32[8,32,128]{2,1,0:T(8,128)S(1)}, ...), condition=%wide.region_9.10_spmd, body=%wide.region_8.9_spmd.sunk | while | flops 442152288 | bytes 46343604 | solution.py:197
  406.4 1.3 convolution_convert_fusion.11
  417.9 1.3 convolution_convert_fusion.10
  469.9 1.3 convolution_convert_fusion.10
  522.0 1.3 convolution_convert_fusion.10
  707.8 2.0 all-gather.1
  709.9 1.7 multiply_divide_fusion
  (1965 shorter events, 347.2 us)
Async XLA Ops:
  0.0 4.3 copy-start.2
  2.7 10.3 %copy-start = (f32[8,32,128]{2,1,0:T(8,128)S(1)}, f32[8,32,128]{2,1,0:T(8,128)}, u32[]{:S(2)}) copy-start(f32[8,32,128]{2,1,0:T(8,128)} %param.9) | copy-start | bytes 393220
  6.7 60.1 %all-to-all-start = ((bf16[4,3,14,14,128]{4,3,2,1,0:T(8,128)(2,1)}), bf16[4,3,14,14,128]{4,3,2,1,0:T(8,128)(2,1)}, u32[]{:S(2)}, u32[]{:S(2)}) async-start(bf16[4,3,14,14,128]{4,3,2,1,0:T(8,128)(2,1)} %scatter_fusion), calls=%async_computation | async-start | bytes 1376256 | tf_op jit(solution)/shard_map/all_to_all | solution.py:176
  13.0 17.0 %copy-start.3 = (bf16[3,1,7,7,7]{4,3,2,1,0:T(8,128)(2,1)S(1)}, bf16[3,1,7,7,7]{4,3,2,1,0:T(8,128)(2,1)}, u32[]{:S(2)}) copy-start(bf16[3,1,7,7,7]{4,3,2,1,0:T(8,128)(2,1)} %param.12) | copy-start | bytes 6178
  13.1 11.8 %collective-permute-start = (bf16[8,6,128]{2,1,0:T(8,128)(2,1)S(1)}, bf16[8,6,128]{2,1,0:T(8,128)(2,1)S(1)}, u32[]{:S(2)}, u32[]{:S(2)}) collective-permute-start(bf16[8,6,128]{2,1,0:T(8,128)(2,1)S(1)} %get-tuple-element.543), channel_id=1, source_target_pairs={{0,4},{4,8},{8,12},{1,5},{5,9},{9,13},{2,6},{6,10},{10,14},{3,7},{... | collective-permute-start | bytes 36872 | tf_op jit(solution)/shard_map/ppermute | solution.py:25
  17.0 7.9 %collective-permute-start.1 = (bf16[8,6,128]{2,1,0:T(8,128)(2,1)S(1)}, bf16[8,6,128]{2,1,0:T(8,128)(2,1)S(1)}, u32[]{:S(2)}, u32[]{:S(2)}) collective-permute-start(bf16[8,6,128]{2,1,0:T(8,128)(2,1)S(1)} %get-tuple-element.544), channel_id=1, source_target_pairs={{4,0},{8,4},{12,8},{5,1},{9,5},{13,9},{6,2},{10,6},{14,10},{7,3},{... | collective-permute-start | bytes 36872 | tf_op jit(solution)/shard_map/ppermute | solution.py:26
  25.0 41.8 %collective-permute-start.2 = (bf16[6,44,128]{2,1,0:T(8,128)(2,1)S(1)}, bf16[6,44,128]{2,1,0:T(8,128)(2,1)S(1)}, u32[]{:S(2)}, u32[]{:S(2)}) collective-permute-start(bf16[6,44,128]{2,1,0:T(8,128)(2,1)S(1)} %get-tuple-element.539), channel_id=1, source_target_pairs={{0,2},{1,3},{4,6},{5,7},{8,10},{9,11},{12,14},{13,15},{16,18},{17,... | collective-permute-start | bytes 202760 | tf_op jit(solution)/shard_map/ppermute | solution.py:25
  28.4 38.3 %collective-permute-start.3 = (bf16[6,44,128]{2,1,0:T(8,128)(2,1)S(1)}, bf16[6,44,128]{2,1,0:T(8,128)(2,1)S(1)}, u32[]{:S(2)}, u32[]{:S(2)}) collective-permute-start(bf16[6,44,128]{2,1,0:T(8,128)(2,1)S(1)} %get-tuple-element.540), channel_id=1, source_target_pairs={{2,0},{3,1},{6,4},{7,5},{10,8},{11,9},{14,12},{15,13},{18,16},{19,... | collective-permute-start | bytes 202760 | tf_op jit(solution)/shard_map/ppermute | solution.py:26
  380.0 14.7 %copy-start.1 = (f32[8,32,128]{2,1,0:T(8,128)}, f32[8,32,128]{2,1,0:T(8,128)S(1)}, u32[]{:S(2)}) copy-start(f32[8,32,128]{2,1,0:T(8,128)S(1)} %reduce_sum.47) | copy-start | bytes 393220
  380.2 2.7 collective-permute-start.4
  381.5 5.6 collective-permute-start.5
  387.2 3.3 collective-permute-start.6
  388.5 6.2 collective-permute-start.7
